TPU v7x, 32 devices: a whole 2x2x4 slice. The times are simulated.
32 devices in a mesh: groups: 2 (over y), seq: 16 (over z, x, core).
Axes of the slice: x: 2, y: 2, z: 4, core: 2. Of those that a mesh axis runs over, the one named last changes fastest.
Arguments:
- key_values: bfloat16 [3, 2048, 8192], P(None, 'seq', 'groups'), parts along dimension 2, may hold values from -14 to 14, as said below
- bases: bfloat16 [3, 2, 1024, 256], replicated, may hold values from -0.1875 to 0.1875
- owner_slots: int32 [3, 64], P(None, ('groups', 'seq')), parts along dimension 1, may hold values from 0 to 15, as said below
Outputs:
- received: bfloat16 [512, 512, 128], P(('groups', 'seq')), parts along dimension 0
- grams: float32 [6, 2, 256, 256], P('groups'), parts along dimension 0
- energies: float32 [6, 2, 1024], P('groups'), parts along dimension 0
There are 2 independent parts, one for each index of `groups`. A program takes and returns all parts, laid end to end along the dimension named above; an argument that names none is the same for every part. Nothing has to cross between parts.
Inputs may be any that keep to these rules, and one draw needn't show every extreme that they name: key_values are finite real values within the range. `owner_slots`: block j of a layer belongs to device j // 2 of seq; the 6 values of one device's blocks over all layers are distinct, so an owner's slot is written at most once; some owner has all 16 slots filled.
All inputs are finite; a program needn't handle non-finite values.
Results may differ from a plain program's by a relative error of at most 0.001.
Values may be sent and summed in bfloat16 or wider, within the bound.
A program may use at most 128 MiB of HBM per device.

v0:
```python
import jax
import jax.numpy as jnp
from jax import lax
from jax.sharding import PartitionSpec as P

REACH = 8
OWNER_SLOT_LIMIT = 2
CAP = 16


def from_behind(block, axis, distance):
    devices = range(lax.axis_size(axis))
    route = [((i - distance) % len(devices), i) for i in devices]
    return lax.ppermute(block, axis, route)


def per_device(key_values, bases, owner_slots):
    dev_count = lax.axis_size("seq")
    layers = key_values.shape[0]
    width = bases.shape[2]
    rank = bases.shape[3]
    tok_dev = key_values.shape[2] // dev_count
    tokens = tok_dev * dev_count
    blk_dev = owner_slots.shape[1]
    blk_rows = tok_dev // blk_dev
    whole = lax.all_to_all(key_values, "seq", split_axis=2, concat_axis=1, tiled=True)
    gram_list = []
    energy_list = []
    block_list = []
    for layer_idx in range(layers):
        slab_rows = whole[layer_idx]
        slab_rows = slab_rows.reshape(2, width, tok_dev)
        basis = bases[layer_idx]
        coeff = jnp.einsum(
            "scr,sct->srt", basis, slab_rows, preferred_element_type=jnp.float32
        ).astype(jnp.bfloat16)
        recon = jnp.einsum("scr,srt->sct", basis, coeff, preferred_element_type=jnp.float32)
        resid = slab_rows.astype(jnp.float32) - recon
        energy_term = jnp.sum(resid * resid, axis=2)
        gram_term = jnp.einsum("srt,sqt->srq", coeff, coeff, preferred_element_type=jnp.float32)
        gram_total, energy_total = lax.psum((gram_term, energy_term), "seq")
        gram_list.append(gram_total / tokens)
        energy_list.append(energy_total / tokens)
        block_list.append(coeff.reshape(2 * rank, blk_dev, blk_rows).transpose(1, 0, 2))
    grams = jnp.stack(gram_list)
    energies = jnp.stack(energy_list)
    unit_count = layers * blk_dev
    units = jnp.stack(block_list).reshape(unit_count, 2 * rank * blk_rows)
    slot_vals = owner_slots.reshape(unit_count)
    one_hot = (slot_vals[:, None] == jnp.arange(CAP, dtype=jnp.int32)[None, :]).astype(jnp.bfloat16)
    outgoing = jnp.einsum("us,uf->sf", one_hot, units, preferred_element_type=jnp.float32).astype(
        jnp.bfloat16
    )
    outgoing = outgoing.reshape(REACH, OWNER_SLOT_LIMIT, 2 * rank, blk_rows)
    arrived = [outgoing[0]]
    for offset in range(1, REACH):
        arrived.append(from_behind(outgoing[offset], "seq", offset))
    buffer_all = jnp.stack(arrived)
    received = buffer_all.reshape(REACH * OWNER_SLOT_LIMIT, 2 * rank, blk_rows)
    return (received, grams, energies)


def solution(mesh):
    in_specs = (P(None, "seq", "groups"), P(), P(None, ("groups", "seq")))
    out_specs = (
        P(("groups", "seq"), None, None),
        P("groups", None, None, None),
        P("groups", None, None),
    )
    return jax.shard_map(
        per_device, mesh=mesh, in_specs=in_specs, out_specs=out_specs, check_vma=False
    )
```

profile of v0, /device:TPU:0, one launch (start us, length us, event | category | flops | bytes accessed | tf_op | source)
XLA Modules:
  0.0 329.7 jit_solution(11468838820563559150)
XLA Ops:
  7.2 7.2 %copy.39 = bf16[3,128,4096]{1,0,2:T(4,128)(2,1)} copy(bf16[3,128,4096]{2,1,0:T(8,128)(2,1)} %param.3) | data formatting | bytes 6291456 | tf_op args[0]
  14.4 7.5 %all-to-all-start = ((bf16[3,128,4096]{1,0,2:T(4,128)(2,1)}), bf16[3,128,4096]{1,0,2:T(4,128)(2,1)}, u32[]{:S(2)}, u32[]{:S(2)}) async-start(bf16[3,128,4096]{1,0,2:T(4,128)(2,1)} %copy.39), calls=%async_computation | async-start | bytes 8388608 | tf_op jit(solution)/shard_map/all_to_all | solution.py:26
  22.0 0.0 all-reduce.4.cloned.1.call-start
  22.0 0.1 copy.37
  22.1 0.1 eq.15
  22.2 77.4 %all-to-all-done = bf16[3,128,4096]{1,0,2:T(4,128)(2,1)} async-done(((bf16[3,128,4096]{1,0,2:T(4,128)(2,1)}), bf16[3,128,4096]{1,0,2:T(4,128)(2,1)}, u32[]{:S(2)}, u32[]{:S(2)}) %all-to-all-start) | async-done | bytes 3145760 | tf_op jit(solution)/shard_map/all_to_all | solution.py:26
  99.6 5.5 %copy.40 = bf16[3,128,16,256]{3,1,2,0:T(8,128)(2,1)S(1)} copy(bf16[3,128,16,256]{1,0,3,2:T(4,128)(2,1)} %bitcast.1) | data formatting | bytes 6291456 | tf_op jit(solution)/shard_map/all_to_all | solution.py:26
  105.2 1.6 fusion.21
  106.8 1.0 copy-done.4
  107.8 0.5 convolution_convert_fusion.2
  108.3 0.6 fusion.3
  108.9 0.1 reshape.45
  109.0 0.6 copy-done.1
  109.5 1.8 convolution_convert_fusion.1
  111.3 1.9 fusion.1
  113.2 0.1 reshape.46
  113.3 1.7 convolution_convert_fusion.3
  115.0 1.8 fusion.5
  116.8 0.1 reshape.44
  116.9 1.1 fusion.22
  118.0 1.1 fusion.23
  119.0 1.1 fusion.24
  120.1 0.1 copy_bitcast_fusion.7
  120.2 0.1 pad_maximum_fusion.1
  120.3 0.9 convolution_convert_fusion
  121.2 1.5 slice_bitcast_fusion
  122.8 0.7 bitcast_dynamic-update-slice_fusion
  123.5 0.8 collective-permute-start
  124.4 6.2 %collective-permute-start.1 = (bf16[2,512,128]{2,1,0:T(8,128)(2,1)S(1)}, bf16[2,512,128]{2,1,0:T(8,128)(2,1)S(1)}, u32[]{:S(2)}, u32[]{:S(2)}) collective-permute-start(bf16[2,512,128]{2,1,0:T(8,128)(2,1)S(1)} %bitcast.153), channel_id=1, source_target_pairs={{14,0},{15,1},{0,2},{1,3},{2,4},{3,5},{4,6},{5,7},{6,8},{7,9},{8,1... | collective-permute-start | bytes 786440 | tf_op jit(solution)/shard_map/ppermute | solution.py:14
  130.7 12.0 %collective-permute-start.2 = (bf16[2,512,128]{2,1,0:T(8,128)(2,1)S(1)}, bf16[2,512,128]{2,1,0:T(8,128)(2,1)S(1)}, u32[]{:S(2)}, u32[]{:S(2)}) collective-permute-start(bf16[2,512,128]{2,1,0:T(8,128)(2,1)S(1)} %bitcast.152), channel_id=1, source_target_pairs={{13,0},{14,1},{15,2},{0,3},{1,4},{2,5},{3,6},{4,7},{5,8},{6,9},{7,... | collective-permute-start | bytes 786440 | tf_op jit(solution)/shard_map/ppermute | solution.py:14
  142.7 0.7 collective-permute-start.3
  143.5 0.2 collective-permute-start.4
  143.6 75.5 %all-reduce = (f32[2,1024]{1,0:T(2,128)S(1)}, f32[2,1024]{1,0:T(2,128)S(1)}, f32[2,1024]{1,0:T(2,128)S(1)}) all-reduce(f32[2,1024]{1,0:T(2,128)S(1)} %fusion.1, f32[2,1024]{1,0:T(2,128)S(1)} %fusion.3, f32[2,1024]{1,0:T(2,128)S(1)} %fusion.5), channel_id=1, replica_groups=mesh['groups'=2,'seq'=16] {'seq'}, use_global_device_ids=true, to_apply=%region_8.0 | all-reduce | flops 6144 | bytes 49152 | tf_op jit(solution)/shard_map/psum | solution.py:41
  219.1 0.6 pad_maximum_fusion.2
  219.9 0.0 all-reduce.4.cloned.1.call-update
  219.9 0.1 collective-permute-start.5
  220.0 0.7 bitcast_dynamic-update-slice_fusion.7
  220.7 0.7 bitcast_dynamic-update-slice_fusion.6
  221.4 0.7 bitcast_dynamic-update-slice_fusion.5
  222.1 0.7 bitcast_dynamic-update-slice_fusion.4
  222.9 0.7 bitcast_dynamic-update-slice_fusion.3
  223.6 16.2 %collective-permute-done.5 = bf16[2,512,128]{2,1,0:T(8,128)(2,1)S(1)} collective-permute-done((bf16[2,512,128]{2,1,0:T(8,128)(2,1)S(1)}, bf16[2,512,128]{2,1,0:T(8,128)(2,1)S(1)}, u32[]{:S(2)}, u32[]{:S(2)}) %collective-permute-start.5) | collective-permute-done | bytes 262176 | tf_op jit(solution)/shard_map/ppermute | solution.py:14
  239.8 0.7 bitcast_dynamic-update-slice_fusion.2
  240.5 0.7 bitcast_dynamic-update-slice_fusion.1
  241.2 78.0 %all-reduce.4.cloned.1.call-done = (f32[2,256,256]{2,1,0:T(8,128)}, f32[2,256,256]{2,1,0:T(8,128)}, f32[2,256,256]{2,1,0:T(8,128)}) async-done(((f32[2,256,256]{2,1,0:T(8,128)}, f32[2,256,256]{2,1,0:T(8,128)}, f32[2,256,256]{2,1,0:T(8,128)}), (f32[2,256,256]{2,1,0:T(8,128)}, f32[2,256,256]{2,1,0:T(8,128)}, f32[2,256,256]{2,1,0:T(8,128)})) %all-reduce.4.cloned.1.call-update) | async-done | bytes 1572880 | tf_op jit(solution)/shard_map/psum | solution.py:41
  319.2 1.1 multiply_bitcast_fusion.2
  320.3 1.3 multiply_bitcast_fusion
  321.6 1.2 pad_maximum_fusion
  (25 shorter events, 0.3 us)
Async XLA Ops:
  14.4 7.6 %copy-start.3 = (s32[3,2]{0,1:T(2,128)S(1)}, s32[3,2]{0,1:T(2,128)}, u32[]{:S(2)}) copy-start(s32[3,2]{0,1:T(2,128)} %param.5) | copy-start | bytes 76
  14.4 85.2 %all-to-all-start = ((bf16[3,128,4096]{1,0,2:T(4,128)(2,1)}), bf16[3,128,4096]{1,0,2:T(4,128)(2,1)}, u32[]{:S(2)}, u32[]{:S(2)}) async-start(bf16[3,128,4096]{1,0,2:T(4,128)(2,1)} %copy.39), calls=%async_computation | async-start | bytes 8388608 | tf_op jit(solution)/shard_map/all_to_all | solution.py:26
  22.0 297.3 %all-reduce.4.cloned.1.call-start = ((), (), s32[]{:S(2)}) async-start(), calls=%async_computation.1 | async-start | bytes 3145728 | tf_op jit(solution)/shard_map/psum | solution.py:41
  105.1 2.6 copy-start.4
  108.3 1.2 copy-start.1
  109.0 2.3 copy-start.2
  111.3 2.0 copy-start
  123.5 96.4 %collective-permute-start = (bf16[2,512,128]{2,1,0:T(8,128)(2,1)S(1)}, bf16[2,512,128]{2,1,0:T(8,128)(2,1)S(1)}, u32[]{:S(2)}, u32[]{:S(2)}) collective-permute-start(bf16[2,512,128]{2,1,0:T(8,128)(2,1)S(1)} %bitcast.154), channel_id=1, source_target_pairs={{15,0},{0,1},{1,2},{2,3},{3,4},{4,5},{5,6},{6,7},{7,8},{8,9},{9,10... | collective-permute-start | bytes 786440 | tf_op jit(solution)/shard_map/ppermute | solution.py:14
  124.4 96.3 %collective-permute-start.1 = (bf16[2,512,128]{2,1,0:T(8,128)(2,1)S(1)}, bf16[2,512,128]{2,1,0:T(8,128)(2,1)S(1)}, u32[]{:S(2)}, u32[]{:S(2)}) collective-permute-start(bf16[2,512,128]{2,1,0:T(8,128)(2,1)S(1)} %bitcast.153), channel_id=1, source_target_pairs={{14,0},{15,1},{0,2},{1,3},{2,4},{3,5},{4,6},{5,7},{6,8},{7,9},{8,1... | collective-permute-start | bytes 786440 | tf_op jit(solution)/shard_map/ppermute | solution.py:14
  130.7 90.7 %collective-permute-start.2 = (bf16[2,512,128]{2,1,0:T(8,128)(2,1)S(1)}, bf16[2,512,128]{2,1,0:T(8,128)(2,1)S(1)}, u32[]{:S(2)}, u32[]{:S(2)}) collective-permute-start(bf16[2,512,128]{2,1,0:T(8,128)(2,1)S(1)} %bitcast.152), channel_id=1, source_target_pairs={{13,0},{14,1},{15,2},{0,3},{1,4},{2,5},{3,6},{4,7},{5,8},{6,9},{7,... | collective-permute-start | bytes 786440 | tf_op jit(solution)/shard_map/ppermute | solution.py:14
  142.7 79.4 %collective-permute-start.3 = (bf16[2,512,128]{2,1,0:T(8,128)(2,1)S(1)}, bf16[2,512,128]{2,1,0:T(8,128)(2,1)S(1)}, u32[]{:S(2)}, u32[]{:S(2)}) collective-permute-start(bf16[2,512,128]{2,1,0:T(8,128)(2,1)S(1)} %bitcast.151), channel_id=1, source_target_pairs={{12,0},{13,1},{14,2},{15,3},{0,4},{1,5},{2,6},{3,7},{4,8},{5,9},{6... | collective-permute-start | bytes 786440 | tf_op jit(solution)/shard_map/ppermute | solution.py:14
  143.5 79.4 %collective-permute-start.4 = (bf16[2,512,128]{2,1,0:T(8,128)(2,1)S(1)}, bf16[2,512,128]{2,1,0:T(8,128)(2,1)S(1)}, u32[]{:S(2)}, u32[]{:S(2)}) collective-permute-start(bf16[2,512,128]{2,1,0:T(8,128)(2,1)S(1)} %bitcast.150), channel_id=1, source_target_pairs={{11,0},{12,1},{13,2},{14,3},{15,4},{0,5},{1,6},{2,7},{3,8},{4,9},{... | collective-permute-start | bytes 786440 | tf_op jit(solution)/shard_map/ppermute | solution.py:14
  219.9 19.9 %collective-permute-start.5 = (bf16[2,512,128]{2,1,0:T(8,128)(2,1)S(1)}, bf16[2,512,128]{2,1,0:T(8,128)(2,1)S(1)}, u32[]{:S(2)}, u32[]{:S(2)}) collective-permute-start(bf16[2,512,128]{2,1,0:T(8,128)(2,1)S(1)} %bitcast.156), channel_id=1, source_target_pairs={{10,0},{11,1},{12,2},{13,3},{14,4},{15,5},{0,6},{1,7},{2,8},{3,9},... | collective-permute-start | bytes 786440 | tf_op jit(solution)/shard_map/ppermute | solution.py:14
  220.7 19.8 %collective-permute-start.6 = (bf16[2,512,128]{2,1,0:T(8,128)(2,1)S(1)}, bf16[2,512,128]{2,1,0:T(8,128)(2,1)S(1)}, u32[]{:S(2)}, u32[]{:S(2)}) collective-permute-start(bf16[2,512,128]{2,1,0:T(8,128)(2,1)S(1)} %bitcast.155), channel_id=1, source_target_pairs={{9,0},{10,1},{11,2},{12,3},{13,4},{14,5},{15,6},{0,7},{1,8},{2,9},... | collective-permute-start | bytes 786440 | tf_op jit(solution)/shard_map/ppermute | solution.py:14
Sparse Core Ops, SparseCore 0:
  220.0 99.1 all-reduce.3
where the time goes:
time: 330 us
  waiting for transfers between devices  172 us (52%)
  blocking collectives  75.5 us (23%)
  starting transfers between devices  27.6 us (8%)
  local copies, waits for them, and re-layouts  24 us (7%)
  between operations  14.3 us (4%)
  matrix products  12.3 us (4%)
  other arithmetic  4.34 us (1%)
    psum x1, waiting for transfers between devices, per_device(): gram_total, energy_total = lax.psum((gram_term, energy_term), 'seq')  78 us
    all_to_all x1, waiting for transfers between devices, per_device(): lax.all_to_all(key_values, 'seq', split_axis=2, concat_axis=1, tiled=True)  77.4 us
    psum x1, blocking collectives, per_device(): gram_total, energy_total = lax.psum((gram_term, energy_term), 'seq')  75.5 us
    ppermute x7, starting transfers between devices, from_behind(): return lax.ppermute(block, axis, route)  20 us
    ppermute x7, waiting for transfers between devices, from_behind(): return lax.ppermute(block, axis, route)  16.2 us
    unnamed x27, local copies, waits for them, and re-layouts  15.8 us
    all_to_all x1, starting transfers between devices, per_device(): lax.all_to_all(key_values, 'seq', split_axis=2, concat_axis=1, tiled=True)  7.54 us
  transfers between devices with their start and end apart: 9, of which 3 were waited for; matrix products, arithmetic and copies ran while one was open for 2% of the time, Pallas kernels for 0%

commit v1 on v0

--- a/solution.py
+++ b/solution.py
@@ -23,7 +23,10 @@
     tokens = tok_dev * dev_count
     blk_dev = owner_slots.shape[1]
     blk_rows = tok_dev // blk_dev
-    whole = lax.all_to_all(key_values, "seq", split_axis=2, concat_axis=1, tiled=True)
+    whole = jnp.concatenate(
+        lax.all_to_all(jnp.stack(jnp.split(key_values, lax.axis_size("seq"), axis=2)), "seq", 0, 0),
+        axis=1,
+    )
     gram_list = []
     energy_list = []
     block_list = []

time: 330 us -> 327 us (level)
  waiting for transfers between devices: 172 us -> 154 us
  local copies, waits for them, and re-layouts: 24 us -> 38.7 us
  starting transfers between devices: 27.6 us -> 23.3 us
    all_to_all x1, waiting for transfers between devices: 77.4 us -> 59.1 us  [per_device(): lax.all_to_all(jnp.stack(jnp.split(key_values, lax.axis_size('seq'), axis...]
    unnamed x27 -> x37, local copies, waits for them, and re-layouts: 15.8 us -> 31.2 us
    another operation x0 -> x4, local copies, waits for them, and re-layouts: none -> 5.57 us  [the longest x3 3.94 us: per_device(): slab_rows = slab_rows.reshape(2, width, tok_dev)]
    all_to_all x1, local copies, waits for them, and re-layouts: 5.5 us -> 0.2 us  [per_device(): lax.all_to_all(jnp.stack(jnp.split(key_values, lax.axis_size('seq'), axis...]
    ppermute x7, starting transfers between devices: 20 us -> 15.8 us  [from_behind(): return lax.ppermute(block, axis, route)]
where the time goes in v1:
time: 327 us; the launch traced here: 326 us
  waiting for transfers between devices  154 us (47%)
  blocking collectives  75.5 us (23%)
  local copies, waits for them, and re-layouts  38.7 us (12%)
  starting transfers between devices  23.3 us (7%)
  matrix products  14.9 us (5%)
  between operations  14.3 us (4%)
  other arithmetic  5.55 us (2%)
    psum x1, waiting for transfers between devices, per_device(): gram_total, energy_total = lax.psum((gram_term, energy_term), 'seq')  78.5 us
    psum x1, blocking collectives, per_device(): gram_total, energy_total = lax.psum((gram_term, energy_term), 'seq')  75.5 us
    all_to_all x1, waiting for transfers between devices, per_device(): lax.all_to_all(jnp.stack(jnp.split(key_values, lax.axis_size('seq'), axis...  59.1 us
    unnamed x37, local copies, waits for them, and re-layouts  31.2 us
    ppermute x7, waiting for transfers between devices, from_behind(): return lax.ppermute(block, axis, route)  16.2 us
    ppermute x7, starting transfers between devices, from_behind(): return lax.ppermute(block, axis, route)  15.8 us
    all_to_all x1, starting transfers between devices, per_device(): lax.all_to_all(jnp.stack(jnp.split(key_values, lax.axis_size('seq'), axis...  7.49 us
  transfers between devices with their start and end apart: 9, of which 3 were waited for; matrix products, arithmetic and copies ran while one was open for 2% of the time, Pallas kernels for 0%

profile of v1, /device:TPU:0, one launch (start us, length us, event | category | flops | bytes accessed | tf_op | source)
XLA Modules:
  0.0 326.0 jit_solution(17006212149676294502)
XLA Ops:
  7.2 1.6 bitcast_dynamic-update-slice_fusion.23
  8.8 1.6 bitcast_dynamic-update-slice_fusion.22
  10.4 1.6 bitcast_dynamic-update-slice_fusion.21
  12.0 1.6 bitcast_dynamic-update-slice_fusion.20
  13.6 1.6 bitcast_dynamic-update-slice_fusion.19
  15.2 1.6 bitcast_dynamic-update-slice_fusion.18
  16.8 1.6 bitcast_dynamic-update-slice_fusion.17
  18.5 1.6 bitcast_dynamic-update-slice_fusion.16
  20.1 1.6 bitcast_dynamic-update-slice_fusion.15
  21.7 1.6 bitcast_dynamic-update-slice_fusion.14
  23.3 1.6 bitcast_dynamic-update-slice_fusion.13
  24.9 1.6 bitcast_dynamic-update-slice_fusion.12
  26.6 1.6 bitcast_dynamic-update-slice_fusion.11
  28.2 1.6 bitcast_dynamic-update-slice_fusion.10
  29.8 1.6 bitcast_dynamic-update-slice_fusion.9
  31.4 1.6 bitcast_dynamic-update-slice_fusion.8
  33.0 7.5 %all-to-all-start = ((bf16[16,3,128,256]{3,2,1,0:T(8,128)(2,1)}), bf16[16,3,128,256]{3,2,1,0:T(8,128)(2,1)S(1)}, u32[]{:S(2)}, u32[]{:S(2)}) async-start(bf16[16,3,128,256]{3,2,1,0:T(8,128)(2,1)} %bitcast_dynamic-update-slice_fusion.8), calls=%async_computation | async-start | bytes 6291456 | tf_op jit(solution)/shard_map/all_to_all | solution.py:27
  40.8 59.1 %all-to-all-done = bf16[16,3,128,256]{3,2,1,0:T(8,128)(2,1)S(1)} async-done(((bf16[16,3,128,256]{3,2,1,0:T(8,128)(2,1)}), bf16[16,3,128,256]{3,2,1,0:T(8,128)(2,1)S(1)}, u32[]{:S(2)}, u32[]{:S(2)}) %all-to-all-start) | async-done | bytes 3145760 | tf_op jit(solution)/shard_map/all_to_all | solution.py:27
  100.3 1.3 copy.36
  101.6 1.7 convolution_convert_fusion.3
  103.4 1.7 convolution_convert_fusion.2
  105.1 1.3 copy.37
  106.4 1.7 convolution_convert_fusion.1
  108.2 1.3 copy.38
  109.5 1.1 fusion.22
  110.6 2.0 fusion.5
  112.7 1.1 fusion.23
  113.7 1.7 fusion.3
  115.5 1.1 fusion.24
  116.6 1.7 fusion.1
  118.9 1.3 pad_maximum_fusion.1
  120.4 0.9 convolution_convert_fusion
  121.3 1.5 slice_bitcast_fusion
  122.8 0.7 bitcast_dynamic-update-slice_fusion
  123.6 0.8 collective-permute-start
  124.4 4.8 %collective-permute-start.1 = (bf16[2,512,128]{2,1,0:T(8,128)(2,1)S(1)}, bf16[2,512,128]{2,1,0:T(8,128)(2,1)S(1)}, u32[]{:S(2)}, u32[]{:S(2)}) collective-permute-start(bf16[2,512,128]{2,1,0:T(8,128)(2,1)S(1)} %bitcast.184), channel_id=1, source_target_pairs={{14,0},{15,1},{0,2},{1,3},{2,4},{3,5},{4,6},{5,7},{6,8},{7,9},{8,1... | collective-permute-start | bytes 786440 | tf_op jit(solution)/shard_map/ppermute | solution.py:14
  129.3 9.2 %collective-permute-start.2 = (bf16[2,512,128]{2,1,0:T(8,128)(2,1)S(1)}, bf16[2,512,128]{2,1,0:T(8,128)(2,1)S(1)}, u32[]{:S(2)}, u32[]{:S(2)}) collective-permute-start(bf16[2,512,128]{2,1,0:T(8,128)(2,1)S(1)} %bitcast.183), channel_id=1, source_target_pairs={{13,0},{14,1},{15,2},{0,3},{1,4},{2,5},{3,6},{4,7},{5,8},{6,9},{7,... | collective-permute-start | bytes 786440 | tf_op jit(solution)/shard_map/ppermute | solution.py:14
  138.5 0.7 collective-permute-start.3
  139.5 75.5 %all-reduce = (f32[2,1024]{1,0:T(2,128)S(1)}, f32[2,1024]{1,0:T(2,128)S(1)}, f32[2,1024]{1,0:T(2,128)S(1)}) all-reduce(f32[2,1024]{1,0:T(2,128)S(1)} %fusion.1, f32[2,1024]{1,0:T(2,128)S(1)} %fusion.3, f32[2,1024]{1,0:T(2,128)S(1)} %fusion.5), channel_id=1, replica_groups=mesh['groups'=2,'seq'=16] {'seq'}, use_global_device_ids=true, to_apply=%region_8.0 | all-reduce | flops 6144 | bytes 49152 | tf_op jit(solution)/shard_map/psum | solution.py:44
  215.8 0.7 bitcast_dynamic-update-slice_fusion.7
  216.5 0.7 bitcast_dynamic-update-slice_fusion.6
  217.2 0.7 bitcast_dynamic-update-slice_fusion.5
  218.0 0.7 bitcast_dynamic-update-slice_fusion.4
  219.4 16.1 %collective-permute-done.5 = bf16[2,512,128]{2,1,0:T(8,128)(2,1)S(1)} collective-permute-done((bf16[2,512,128]{2,1,0:T(8,128)(2,1)S(1)}, bf16[2,512,128]{2,1,0:T(8,128)(2,1)S(1)}, u32[]{:S(2)}, u32[]{:S(2)}) %collective-permute-start.5) | collective-permute-done | bytes 262176 | tf_op jit(solution)/shard_map/ppermute | solution.py:14
  237.0 78.5 %all-reduce.4.cloned.1.call-done = (f32[2,256,256]{2,1,0:T(8,128)}, f32[2,256,256]{2,1,0:T(8,128)}, f32[2,256,256]{2,1,0:T(8,128)}) async-done(((f32[2,256,256]{2,1,0:T(8,128)}, f32[2,256,256]{2,1,0:T(8,128)}, f32[2,256,256]{2,1,0:T(8,128)}), (f32[2,256,256]{2,1,0:T(8,128)}, f32[2,256,256]{2,1,0:T(8,128)}, f32[2,256,256]{2,1,0:T(8,128)})) %all-reduce.4.cloned.1.call-update) | async-done | bytes 1572880 | tf_op jit(solution)/shard_map/psum | solution.py:44
  315.5 1.1 multiply_bitcast_fusion.2
  316.6 1.3 multiply_bitcast_fusion
  317.9 1.2 pad_maximum_fusion
  (41 shorter events, 4.7 us)
Async XLA Ops:
  33.0 7.5 %copy-start.2 = (s32[3,2]{0,1:T(2,128)S(1)}, s32[3,2]{0,1:T(2,128)}, u32[]{:S(2)}) copy-start(s32[3,2]{0,1:T(2,128)} %param.5) | copy-start | bytes 76
  33.0 66.9 %all-to-all-start = ((bf16[16,3,128,256]{3,2,1,0:T(8,128)(2,1)}), bf16[16,3,128,256]{3,2,1,0:T(8,128)(2,1)S(1)}, u32[]{:S(2)}, u32[]{:S(2)}) async-start(bf16[16,3,128,256]{3,2,1,0:T(8,128)(2,1)} %bitcast_dynamic-update-slice_fusion.8), calls=%async_computation | async-start | bytes 6291456 | tf_op jit(solution)/shard_map/all_to_all | solution.py:27
  40.5 275.0 %all-reduce.4.cloned.1.call-start = ((), (), s32[]{:S(2)}) async-start(), calls=%async_computation.1 | async-start | bytes 3145728 | tf_op jit(solution)/shard_map/psum | solution.py:44
  109.5 4.2 %copy-start.1 = (bf16[2,1024,256]{1,2,0:T(8,128)(2,1)S(1)}, bf16[2,1024,256]{1,2,0:T(8,128)(2,1)}, u32[]{:S(2)}) copy-start(bf16[2,1024,256]{1,2,0:T(8,128)(2,1)} %copy.37) | copy-start | bytes 3145732
  112.6 3.9 %copy-start = (bf16[2,1024,256]{1,2,0:T(8,128)(2,1)S(1)}, bf16[2,1024,256]{1,2,0:T(8,128)(2,1)}, u32[]{:S(2)}) copy-start(bf16[2,1024,256]{1,2,0:T(8,128)(2,1)} %copy.38) | copy-start | bytes 3145732
  123.6 92.1 %collective-permute-start = (bf16[2,512,128]{2,1,0:T(8,128)(2,1)S(1)}, bf16[2,512,128]{2,1,0:T(8,128)(2,1)S(1)}, u32[]{:S(2)}, u32[]{:S(2)}) collective-permute-start(bf16[2,512,128]{2,1,0:T(8,128)(2,1)S(1)} %bitcast.185), channel_id=1, source_target_pairs={{15,0},{0,1},{1,2},{2,3},{3,4},{4,5},{5,6},{6,7},{7,8},{8,9},{9,10... | collective-permute-start | bytes 786440 | tf_op jit(solution)/shard_map/ppermute | solution.py:14
  124.4 92.1 %collective-permute-start.1 = (bf16[2,512,128]{2,1,0:T(8,128)(2,1)S(1)}, bf16[2,512,128]{2,1,0:T(8,128)(2,1)S(1)}, u32[]{:S(2)}, u32[]{:S(2)}) collective-permute-start(bf16[2,512,128]{2,1,0:T(8,128)(2,1)S(1)} %bitcast.184), channel_id=1, source_target_pairs={{14,0},{15,1},{0,2},{1,3},{2,4},{3,5},{4,6},{5,7},{6,8},{7,9},{8,1... | collective-permute-start | bytes 786440 | tf_op jit(solution)/shard_map/ppermute | solution.py:14
  129.3 87.9 %collective-permute-start.2 = (bf16[2,512,128]{2,1,0:T(8,128)(2,1)S(1)}, bf16[2,512,128]{2,1,0:T(8,128)(2,1)S(1)}, u32[]{:S(2)}, u32[]{:S(2)}) collective-permute-start(bf16[2,512,128]{2,1,0:T(8,128)(2,1)S(1)} %bitcast.183), channel_id=1, source_target_pairs={{13,0},{14,1},{15,2},{0,3},{1,4},{2,5},{3,6},{4,7},{5,8},{6,9},{7,... | collective-permute-start | bytes 786440 | tf_op jit(solution)/shard_map/ppermute | solution.py:14
  138.5 79.4 %collective-permute-start.3 = (bf16[2,512,128]{2,1,0:T(8,128)(2,1)S(1)}, bf16[2,512,128]{2,1,0:T(8,128)(2,1)S(1)}, u32[]{:S(2)}, u32[]{:S(2)}) collective-permute-start(bf16[2,512,128]{2,1,0:T(8,128)(2,1)S(1)} %bitcast.182), channel_id=1, source_target_pairs={{12,0},{13,1},{14,2},{15,3},{0,4},{1,5},{2,6},{3,7},{4,8},{5,9},{6... | collective-permute-start | bytes 786440 | tf_op jit(solution)/shard_map/ppermute | solution.py:14
  139.3 79.4 %collective-permute-start.4 = (bf16[2,512,128]{2,1,0:T(8,128)(2,1)S(1)}, bf16[2,512,128]{2,1,0:T(8,128)(2,1)S(1)}, u32[]{:S(2)}, u32[]{:S(2)}) collective-permute-start(bf16[2,512,128]{2,1,0:T(8,128)(2,1)S(1)} %bitcast.181), channel_id=1, source_target_pairs={{11,0},{12,1},{13,2},{14,3},{15,4},{0,5},{1,6},{2,7},{3,8},{4,9},{... | collective-permute-start | bytes 786440 | tf_op jit(solution)/shard_map/ppermute | solution.py:14
  215.7 19.8 %collective-permute-start.5 = (bf16[2,512,128]{2,1,0:T(8,128)(2,1)S(1)}, bf16[2,512,128]{2,1,0:T(8,128)(2,1)S(1)}, u32[]{:S(2)}, u32[]{:S(2)}) collective-permute-start(bf16[2,512,128]{2,1,0:T(8,128)(2,1)S(1)} %bitcast.187), channel_id=1, source_target_pairs={{10,0},{11,1},{12,2},{13,3},{14,4},{15,5},{0,6},{1,7},{2,8},{3,9},... | collective-permute-start | bytes 786440 | tf_op jit(solution)/shard_map/ppermute | solution.py:14
  216.5 19.8 %collective-permute-start.6 = (bf16[2,512,128]{2,1,0:T(8,128)(2,1)S(1)}, bf16[2,512,128]{2,1,0:T(8,128)(2,1)S(1)}, u32[]{:S(2)}, u32[]{:S(2)}) collective-permute-start(bf16[2,512,128]{2,1,0:T(8,128)(2,1)S(1)} %bitcast.186), channel_id=1, source_target_pairs={{9,0},{10,1},{11,2},{12,3},{13,4},{14,5},{15,6},{0,7},{1,8},{2,9},... | collective-permute-start | bytes 786440 | tf_op jit(solution)/shard_map/ppermute | solution.py:14
Sparse Core Ops, SparseCore 0:
  215.8 99.6 all-reduce.3
